TPU v7x, 128 devices: a whole 4x4x4 slice. The times are simulated.
128 devices in a mesh: walk: 16 (over x, z), pan: 8 (over y, core).
Axes of the slice: x: 4, y: 4, z: 4, core: 2. Of those that a mesh axis runs over, the one named last changes fastest.
Arguments:
- dlog: bfloat16 [32768, 4096], P('walk', 'pan'), may hold values from 0 to 2
- dener: bfloat16 [32768, 4096], P('walk', 'pan'), may hold values from -0.5 to 2.5
- energy: float32 [32768], P('walk'), may hold values from -3 to -1
- mask: int32 [16], replicated, may hold values 0 or 1
- owner: int32 [16], replicated, may hold values from 0 to 15, each once
Outputs:
- correlation: float32 [4096, 4096], P('walk', 'pan')
- hamilton: float32 [4096, 4096], P('walk', 'pan')
Inputs may be any that keep to these rules, and one draw needn't show every extreme that they name: `owner`: each block number appears once.
All inputs are finite; a program needn't handle non-finite values.
Results may differ from a plain program's by a relative error of at most 0.005.
Values may be sent and summed in bfloat16 or wider, within the bound.
A program may use at most 128 MiB of HBM per device.

v0:
```python
import jax
import jax.numpy as jnp
from jax import lax
from jax.sharding import PartitionSpec as P

BLOCK = 256


def per_device(dlog, dener, energy, mask, owner):
    wdev, width = dlog.shape
    total = wdev * lax.axis_size("walk")
    full = width * lax.axis_size("pan")
    nblocks = full // BLOCK
    first = lax.axis_index("pan") * (width // BLOCK)
    local_mask = lax.dynamic_slice_in_dim(mask, first, width // BLOCK)
    colmask = jnp.repeat(local_mask, BLOCK).astype(jnp.float32)
    om = dlog.astype(jnp.float32) * colmask
    gm = dener.astype(jnp.float32) * colmask
    osum, gsum, esum = lax.psum((jnp.sum(om, 0), jnp.sum(gm, 0), jnp.sum(energy)), "walk")
    ocf = om - osum / total
    oc = ocf.astype(jnp.bfloat16)
    hc = ((energy - esum / total)[:, None] * ocf + gm - gsum / total).astype(jnp.bfloat16)
    gathered = lax.all_gather(oc, "pan", axis=1, tiled=True)
    ordered = jnp.take(gathered.reshape(wdev, nblocks, BLOCK), owner, axis=1).reshape(wdev, full)
    right_side = jnp.concatenate([oc, hc], 1)
    dims = (((0,), (0,)), ((), ()))
    terms = lax.dot_general(ordered, right_side, dims, preferred_element_type=jnp.float32)
    shares = lax.psum_scatter(terms, "walk", scatter_dimension=0, tiled=True)
    shares = shares / total
    return (shares[:, :width], shares[:, width:])


def solution(mesh):
    return jax.shard_map(
        per_device,
        mesh=mesh,
        in_specs=(P("walk", "pan"), P("walk", "pan"), P("walk"), P(), P()),
        out_specs=(P("walk", "pan"), P("walk", "pan")),
        check_vma=False,
    )
```

profile of v0, /device:TPU:1, one launch (start us, length us, event | category | flops | bytes accessed | tf_op | source)
XLA Modules:
  0.0 329.0 jit_solution(5466082891426086491)
XLA Ops:
  7.2 0.0 copy-start.3
  7.2 0.0 copy-start
  7.2 0.0 all-gather.2.cloned.1.call-start
  7.2 0.9 dynamic-slice_convert_fusion
  8.1 0.1 broadcast_bitcast_fusion
  8.2 1.3 reduce_sum.28
  9.5 3.1 fusion.4
  12.6 36.5 %all-reduce = (f32[512]{0:T(512)S(1)}, f32[512]{0:T(512)S(1)}, f32[]{:T(128)}) all-reduce(f32[512]{0:T(512)S(1)} %get-tuple-element.3, f32[512]{0:T(512)S(1)} %get-tuple-element.2, f32[]{:T(128)} %reduce_sum.28), channel_id=1, replica_groups=mesh['walk'=16,'pan'=8] {'walk'}, use_global_device_ids=true, to_apply=%region_1.0 | all-reduce | flops 1025 | bytes 8200 | tf_op jit(solution)/shard_map/psum | solution.py:19
  49.7 0.0 copy-done.3
  49.7 0.0 copy-done
  49.7 0.0 copy-start.4
  49.8 3.9 %subtract_convert_fusion = (bf16[2048,512]{1,0:T(8,128)(2,1)}, bf16[2048,512]{1,0:T(8,128)(2,1)}) fusion(bf16[2048,512]{1,0:T(8,128)(2,1)S(1)} %copy-done, bf16[2048,512]{1,0:T(8,128)(2,1)} %param.5, f32[512]{0:T(512)S(1)} %get-tuple-element.11, f32[2048]{0:T(1024)S(1)} %broadcast_subtract_fusion, f32[512]{0:T(512)S(1)} %get-tuple-element.12, f32[512]{0:T(512)S(1)} %bitcast.11), kind=kLoop, calls=%fused_computation.6 | loop fusion | flops 10485760 | bytes 8402944 | tf_op jit(solution)/shard_map/convert_element_type | solution.py:22
  53.6 0.0 all-gather.2.cloned.1.call-update
  53.7 0.0 reduce-scatter.2.cloned.1.call-start
  53.7 0.0 copy-done.4
  53.7 0.1 broadcast_in_dim.24
  53.9 89.0 %all-gather.2.cloned.1.call-done = bf16[2048,4096]{1,0:T(8,128)(2,1)} async-done(((bf16[2048,512]{1,0:T(8,128)(2,1)}), bf16[2048,4096]{1,0:T(8,128)(2,1)}) %all-gather.2.cloned.1.call-update) | async-done | bytes 16777232 | tf_op jit(solution)/shard_map/all_gather | solution.py:23
  142.8 22.6 %copy.7 = bf16[2048,4096]{0,1:T(8,128)(2,1)} copy(bf16[2048,4096]{1,0:T(8,128)(2,1)} %all-gather.2.cloned.1.call-done) | data formatting | bytes 33554432 | tf_op jit(solution)/shard_map/all_gather | solution.py:23
  165.4 13.0 %gather_fusion = bf16[16,2048,256]{1,2,0:T(8,128)(2,1)} fusion(bf16[2048,16,256]{0,2,1:T(8,128)(2,1)} %bitcast.9, s32[1024]{0:T(1024)S(1)} %pad_clamp_fusion), kind=kCustom, calls=%fused_computation | custom fusion | bytes 33554496 | tf_op jit(solution)/shard_map/jit(_take)/gather | solution.py:24
  178.4 0.0 copy-start.1
  178.4 0.0 copy-start.2
  178.4 9.5 %bitcast_select_fusion = bf16[2048,4096]{0,1:T(8,128)(2,1)S(1)} fusion(bf16[16,2048,256]{1,2,0:T(8,128)(2,1)} %gather_fusion, pred[4096]{0:T(1024)(128)(4,1)S(1)} %broadcast_in_dim.25), kind=kLoop, calls=%fused_computation.1 | loop fusion | flops 8388608 | bytes 33558528 | tf_op jit(solution)/shard_map/jit(_take)/select_n | solution.py:24
  188.0 0.0 copy-done.1
  188.0 0.0 copy-done.2
  188.0 20.8 %fusion = f32[4096,1024]{1,0:T(8,128)} fusion(bf16[2048,4096]{0,1:T(8,128)(2,1)S(1)} %bitcast_select_fusion, bf16[2048,512]{1,0:T(8,128)(2,1)S(1)} %copy-done.2, bf16[2048,512]{1,0:T(8,128)(2,1)S(1)} %copy-done.1), kind=kOutput, calls=%fused_computation.2 | convolution fusion | flops 17188257792 | bytes 37748736 | tf_op jit(solution)/shard_map/dot_general | solution.py:27
  208.8 0.0 reduce-scatter.2.cloned.1.call-update
  208.8 111.0 %reduce-scatter.2.cloned.1.call-done = f32[256,1024]{1,0:T(8,128)} async-done(((f32[4096,1024]{1,0:T(8,128)}), f32[256,1024]{1,0:T(8,128)}) %reduce-scatter.2.cloned.1.call-update) | async-done | bytes 1048592 | tf_op jit(solution)/shard_map/reduce_scatter | solution.py:28
  319.8 1.3 broadcast_multiply_fusion
  321.1 1.0 fusion.9
  (7 shorter events, 0.0 us)
Async XLA Ops:
  7.2 42.5 %copy-start.3 = (f32[2048]{0:T(1024)S(1)}, f32[2048]{0:T(1024)}, u32[]{:S(2)}) copy-start(f32[2048]{0:T(1024)} %param.7) | copy-start | bytes 24580
  7.2 42.6 %copy-start = (bf16[2048,512]{1,0:T(8,128)(2,1)S(1)}, bf16[2048,512]{1,0:T(8,128)(2,1)}, u32[]{:S(2)}) copy-start(bf16[2048,512]{1,0:T(8,128)(2,1)} %param.6) | copy-start | bytes 6291460
  7.2 135.6 %all-gather.2.cloned.1.call-start = ((), (), s32[]{:S(2)}) async-start(), calls=%async_computation.1 | async-start | bytes 18874368 | tf_op jit(solution)/shard_map/all_gather | solution.py:23
  49.7 4.0 %copy-start.4 = (s32[16]{0:T(128)S(1)}, s32[16]{0:T(128)}, u32[]{:S(2)}) copy-start(s32[16]{0:T(128)} %param.9) | copy-start | bytes 196
  53.7 266.1 %reduce-scatter.2.cloned.1.call-start = ((), (), s32[]{:S(2)}) async-start(), calls=%async_computation.2 | async-start | bytes 17825792 | tf_op jit(solution)/shard_map/reduce_scatter | solution.py:28
  178.4 9.6 %copy-start.1 = (bf16[2048,512]{1,0:T(8,128)(2,1)S(1)}, bf16[2048,512]{1,0:T(8,128)(2,1)}, u32[]{:S(2)}) copy-start(bf16[2048,512]{1,0:T(8,128)(2,1)} %get-tuple-element.8) | copy-start | bytes 6291460
  178.4 9.6 %copy-start.2 = (bf16[2048,512]{1,0:T(8,128)(2,1)S(1)}, bf16[2048,512]{1,0:T(8,128)(2,1)}, u32[]{:S(2)}) copy-start(bf16[2048,512]{1,0:T(8,128)(2,1)} %get-tuple-element.7) | copy-start | bytes 6291460
Sparse Core Ops, SparseCore 0:
  53.8 88.9 all-gather.1
  209.0 110.7 reduce-scatter.1
where the time goes:
time: 330 us; the launch traced here: 329 us
  waiting for transfers between devices  200 us (61%)
  local copies, waits for them, and re-layouts  36.8 us (11%)
  blocking collectives  36.5 us (11%)
  matrix products  20.8 us (6%)
  other arithmetic  20.1 us (6%)
  between operations  14.8 us (4%)
    reduce_scatter x1, waiting for transfers between devices, per_device(): shares = lax.psum_scatter(terms, 'walk', scatter_dimension=0, tiled=True)  111 us
    all_gather x1, waiting for transfers between devices, per_device(): gathered = lax.all_gather(oc, 'pan', axis=1, tiled=True)  89 us
    psum x1, blocking collectives, per_device(): lax.psum((jnp.sum(om, 0), jnp.sum(gm, 0), jnp.sum(energy)), 'walk')  36.5 us
    all_gather x1, local copies, waits for them, and re-layouts, per_device(): gathered = lax.all_gather(oc, 'pan', axis=1, tiled=True)  22.6 us
    dot_general x1, matrix products, per_device(): lax.dot_general(ordered, right_side, dims, preferred_element_type=jnp.flo...  20.8 us
    gather x1, local copies, waits for them, and re-layouts, per_device(): jnp.take(gathered.reshape(wdev, nblocks, BLOCK), owner, axis=1)  13 us
    select_n x2, other arithmetic, per_device(): jnp.take(gathered.reshape(wdev, nblocks, BLOCK), owner, axis=1)  9.55 us
  transfers between devices with their start and end apart: 2, of which 2 were waited for; matrix products, arithmetic and copies ran while one was open for 0% of the time, Pallas kernels for 0%

commit v1 on v0

--- a/solution.py
+++ b/solution.py
@@ -20,7 +20,9 @@
     ocf = om - osum / total
     oc = ocf.astype(jnp.bfloat16)
     hc = ((energy - esum / total)[:, None] * ocf + gm - gsum / total).astype(jnp.bfloat16)
-    gathered = lax.all_gather(oc, "pan", axis=1, tiled=True)
+    gathered = jnp.concatenate(
+        lax.all_to_all(jnp.stack([oc] * lax.axis_size("pan")), "pan", 0, 0), axis=1
+    )
     ordered = jnp.take(gathered.reshape(wdev, nblocks, BLOCK), owner, axis=1).reshape(wdev, full)
     right_side = jnp.concatenate([oc, hc], 1)
     dims = (((0,), (0,)), ((), ()))

time: 330 us -> 418 us (1.27)
  waiting for transfers between devices: 200 us -> 289 us
  starting transfers between devices: 0.08 us -> 13.7 us
  local copies, waits for them, and re-layouts: 36.8 us -> 23.2 us
    all_to_all x0 -> x1, waiting for transfers between devices: none -> 183 us  [per_device(): lax.all_to_all(jnp.stack([oc] * lax.axis_size('pan')), 'pan', 0, 0)]
    all_gather x1 -> x0, waiting for transfers between devices: 89 us -> none  [per_device(): gathered = lax.all_gather(oc, 'pan', axis=1, tiled=True)]
    all_gather x1 -> x0, local copies, waits for them, and re-layouts: 22.6 us -> none  [per_device(): gathered = lax.all_gather(oc, 'pan', axis=1, tiled=True)]
    all_to_all x0 -> x1, starting transfers between devices: none -> 13.7 us  [per_device(): lax.all_to_all(jnp.stack([oc] * lax.axis_size('pan')), 'pan', 0, 0)]
    another operation x0 -> x1, local copies, waits for them, and re-layouts: none -> 6.01 us  [per_device(): jnp.stack([oc] * lax.axis_size('pan'))]
    reduce_scatter x1, waiting for transfers between devices: 111 us -> 105 us  [per_device(): shares = lax.psum_scatter(terms, 'walk', scatter_dimension=0, tiled=True)]
where the time goes in v1:
time: 418 us
  waiting for transfers between devices  289 us (69%)
  blocking collectives  36.5 us (9%)
  local copies, waits for them, and re-layouts  23.2 us (6%)
  matrix products  20.8 us (5%)
  other arithmetic  20.1 us (5%)
  between operations  14.8 us (4%)
  starting transfers between devices  13.7 us (3%)
    all_to_all x1, waiting for transfers between devices, per_device(): lax.all_to_all(jnp.stack([oc] * lax.axis_size('pan')), 'pan', 0, 0)  183 us
    reduce_scatter x1, waiting for transfers between devices, per_device(): shares = lax.psum_scatter(terms, 'walk', scatter_dimension=0, tiled=True)  105 us
    psum x1, blocking collectives, per_device(): lax.psum((jnp.sum(om, 0), jnp.sum(gm, 0), jnp.sum(energy)), 'walk')  36.5 us
    dot_general x1, matrix products, per_device(): lax.dot_general(ordered, right_side, dims, preferred_element_type=jnp.flo...  20.8 us
    all_to_all x1, starting transfers between devices, per_device(): lax.all_to_all(jnp.stack([oc] * lax.axis_size('pan')), 'pan', 0, 0)  13.7 us
    gather x1, local copies, waits for them, and re-layouts, per_device(): jnp.take(gathered.reshape(wdev, nblocks, BLOCK), owner, axis=1)  13 us
    select_n x2, other arithmetic, per_device(): jnp.take(gathered.reshape(wdev, nblocks, BLOCK), owner, axis=1)  9.55 us
  transfers between devices with their start and end apart: 2, of which 2 were waited for; matrix products, arithmetic and copies ran while one was open for 0% of the time, Pallas kernels for 0%

profile of v1, /device:TPU:1, one launch (start us, length us, event | category | flops | bytes accessed | tf_op | source)
XLA Modules:
  0.0 418.0 jit_solution(11198472243756360185)
XLA Ops:
  7.2 0.0 copy-start.3
  7.2 0.0 copy-start
  7.2 0.9 dynamic-slice_convert_fusion
  8.1 0.1 broadcast_bitcast_fusion
  8.2 1.3 reduce_sum.28
  9.5 3.1 fusion.4
  12.5 36.5 %all-reduce = (f32[512]{0:T(512)S(1)}, f32[512]{0:T(512)S(1)}, f32[]{:T(128)}) all-reduce(f32[512]{0:T(512)S(1)} %get-tuple-element.3, f32[512]{0:T(512)S(1)} %get-tuple-element.2, f32[]{:T(128)} %reduce_sum.28), channel_id=1, replica_groups=mesh['walk'=16,'pan'=8] {'walk'}, use_global_device_ids=true, to_apply=%region_1.0 | all-reduce | flops 1025 | bytes 8200 | tf_op jit(solution)/shard_map/psum | solution.py:19
  49.7 0.0 copy-done.3
  49.7 0.0 copy-done
  49.7 3.9 subtract_convert_fusion
  53.6 2.9 copy.7
  56.5 6.0 %stack.2 = bf16[8,2048,512]{1,2,0:T(8,128)(2,1)} broadcast(bf16[2048,512]{0,1:T(8,128)(2,1)S(1)} %copy.7), dimensions={1,2} | broadcast | bytes 18874368 | tf_op jit(solution)/shard_map/stack | solution.py:24
  62.5 0.0 copy-start.4
  62.6 13.7 %all-to-all-start = ((bf16[8,2048,512]{1,2,0:T(8,128)(2,1)}), bf16[8,2048,512]{1,2,0:T(8,128)(2,1)}, u32[]{:S(2)}, u32[]{:S(2)}) async-start(bf16[8,2048,512]{1,2,0:T(8,128)(2,1)} %stack.2), calls=%async_computation | async-start | bytes 33554432 | tf_op jit(solution)/shard_map/all_to_all | solution.py:24
  76.2 0.0 reduce-scatter.2.cloned.1.call-start
  76.2 0.0 copy-done.4
  76.2 0.1 broadcast_in_dim.24
  76.3 183.5 %all-to-all-done = bf16[8,2048,512]{1,2,0:T(8,128)(2,1)} async-done(((bf16[8,2048,512]{1,2,0:T(8,128)(2,1)}), bf16[8,2048,512]{1,2,0:T(8,128)(2,1)}, u32[]{:S(2)}, u32[]{:S(2)}) %all-to-all-start) | async-done | bytes 16777248 | tf_op jit(solution)/shard_map/all_to_all | solution.py:24
  259.8 13.0 %gather_fusion = bf16[16,2048,256]{1,2,0:T(8,128)(2,1)} fusion(bf16[2048,16,256]{0,2,1:T(8,128)(2,1)} %bitcast.1, s32[1024]{0:T(1024)S(1)} %pad_clamp_fusion), kind=kCustom, calls=%fused_computation | custom fusion | bytes 33554496 | tf_op jit(solution)/shard_map/jit(_take)/gather | solution.py:26
  272.8 0.0 copy-start.1
  272.9 0.0 copy-start.2
  272.9 9.5 %bitcast_select_fusion = bf16[2048,4096]{0,1:T(8,128)(2,1)S(1)} fusion(bf16[16,2048,256]{1,2,0:T(8,128)(2,1)} %gather_fusion, pred[4096]{0:T(1024)(128)(4,1)S(1)} %broadcast_in_dim.25), kind=kLoop, calls=%fused_computation.1 | loop fusion | flops 8388608 | bytes 33558528 | tf_op jit(solution)/shard_map/jit(_take)/select_n | solution.py:26
  282.4 0.0 copy-done.1
  282.4 0.0 copy-done.2
  282.4 20.8 %fusion = f32[4096,1024]{1,0:T(8,128)} fusion(bf16[2048,4096]{0,1:T(8,128)(2,1)S(1)} %bitcast_select_fusion, bf16[2048,512]{1,0:T(8,128)(2,1)S(1)} %copy-done.2, bf16[2048,512]{1,0:T(8,128)(2,1)S(1)} %copy-done.1), kind=kOutput, calls=%fused_computation.2 | convolution fusion | flops 17188257792 | bytes 37748736 | tf_op jit(solution)/shard_map/dot_general | solution.py:29
  303.3 0.0 reduce-scatter.2.cloned.1.call-update
  303.3 105.4 %reduce-scatter.2.cloned.1.call-done = f32[256,1024]{1,0:T(8,128)} async-done(((f32[4096,1024]{1,0:T(8,128)}), f32[256,1024]{1,0:T(8,128)}) %reduce-scatter.2.cloned.1.call-update) | async-done | bytes 1048592 | tf_op jit(solution)/shard_map/reduce_scatter | solution.py:30
  408.7 1.3 broadcast_multiply_fusion
  410.1 1.0 fusion.9
  (7 shorter events, 0.0 us)
Async XLA Ops:
  7.2 42.5 %copy-start.3 = (f32[2048]{0:T(1024)S(1)}, f32[2048]{0:T(1024)}, u32[]{:S(2)}) copy-start(f32[2048]{0:T(1024)} %param.7) | copy-start | bytes 24580
  7.2 42.5 %copy-start = (bf16[2048,512]{1,0:T(8,128)(2,1)S(1)}, bf16[2048,512]{1,0:T(8,128)(2,1)}, u32[]{:S(2)}) copy-start(bf16[2048,512]{1,0:T(8,128)(2,1)} %param.6) | copy-start | bytes 6291460
  62.5 13.7 %copy-start.4 = (s32[16]{0:T(128)S(1)}, s32[16]{0:T(128)}, u32[]{:S(2)}) copy-start(s32[16]{0:T(128)} %param.9) | copy-start | bytes 196
  62.6 197.3 %all-to-all-start = ((bf16[8,2048,512]{1,2,0:T(8,128)(2,1)}), bf16[8,2048,512]{1,2,0:T(8,128)(2,1)}, u32[]{:S(2)}, u32[]{:S(2)}) async-start(bf16[8,2048,512]{1,2,0:T(8,128)(2,1)} %stack.2), calls=%async_computation | async-start | bytes 33554432 | tf_op jit(solution)/shard_map/all_to_all | solution.py:24
  76.2 332.5 %reduce-scatter.2.cloned.1.call-start = ((), (), s32[]{:S(2)}) async-start(), calls=%async_computation.2 | async-start | bytes 17825792 | tf_op jit(solution)/shard_map/reduce_scatter | solution.py:30
  272.8 9.6 %copy-start.1 = (bf16[2048,512]{1,0:T(8,128)(2,1)S(1)}, bf16[2048,512]{1,0:T(8,128)(2,1)}, u32[]{:S(2)}) copy-start(bf16[2048,512]{1,0:T(8,128)(2,1)} %get-tuple-element.8) | copy-start | bytes 6291460
  272.9 9.6 %copy-start.2 = (bf16[2048,512]{1,0:T(8,128)(2,1)S(1)}, bf16[2048,512]{1,0:T(8,128)(2,1)}, u32[]{:S(2)}) copy-start(bf16[2048,512]{1,0:T(8,128)(2,1)} %get-tuple-element.7) | copy-start | bytes 6291460
Sparse Core Ops, SparseCore 0:
  303.4 105.2 reduce-scatter.1
